TPU v7x, 1024 devices: a whole 4x4x32 slice. The times are simulated.
1024 devices in a mesh: row: 16 (over x_hi, y, core), pitch: 32 (over z), span: 2 (over x_lo).
Axes of the slice: x: 4 (x_hi: 2, x_lo: 2; x = x_hi * 2 + x_lo), y: 4, z: 32, core: 2. Of those that a mesh axis runs over, the one named last changes fastest.
Arguments:
- outlet: bfloat16 [16, 2, 5, 1024, 4096], P('row', None, None, 'span', 'pitch'), may hold values from -6 to 6
- remap_weight: bfloat16 [1024, 896], P('span'), may hold values from -0.4375 to 0.4375
- band_start: int32 [896], replicated, may hold values from 0 to 832, as said below
- blade_counts: int32 [2], replicated, may hold values from 12 to 60
- mode_orders: int32 [64, 2], replicated, may hold values from -4 to 4
Outputs:
- stator_inlet: bfloat16 [16, 2, 5, 896, 4096], P('row', None, None, 'span', 'pitch')
Inputs may be any that keep to these rules, and one draw needn't show every extreme that they name: Stator radial row m draws from rotor radial rows band_start[m] to band_start[m] + 191; band_start[m] lies within 6 rows of m * 832 / 895, band_start[0] = 0 and band_start[895] = 832.
All inputs are finite; a program needn't handle non-finite values.
Results may differ from a plain program's by a relative error of at most 0.0068.
Values may be sent and summed in bfloat16 or wider, within the bound.
A program may use at most 32 MiB of HBM per device.

v0:
```python
import math

import jax
import jax.numpy as jnp
from jax import lax
from jax.sharding import PartitionSpec as P

BAND = 192


def passed_along(value, axis, steps):
    count = lax.axis_size(axis)
    pairs = [(source, (source + steps) % count) for source in range(count)]
    return lax.ppermute(value, axis, pairs)


def pitch_table(wavenumber, first_row, number, total_pitch):
    circumferential_coordinates = first_row + jnp.arange(number, dtype=jnp.int32)
    angular_offsets = jnp.mod(
        circumferential_coordinates[:, None] * wavenumber[None, :], total_pitch
    )
    angles = 2.0 * math.pi / total_pitch * angular_offsets.astype(jnp.float32)
    return jnp.stack([jnp.cos(angles), jnp.sin(angles)], axis=2).reshape(
        number, 2 * wavenumber.shape[0]
    )


def body(outlet, remap_weight, band_start, blade_counts, mode_orders):
    row_count = lax.axis_size("row")
    pitch_count = lax.axis_size("pitch")
    cascade_index_map = lax.axis_index("row")
    pitch_at = lax.axis_index("pitch")
    span_at = lax.axis_index("span")
    planes = outlet[0]
    drawn_cases, fields, rad_loc, pitch_location = planes.shape
    total_pitch = pitch_location * pitch_count
    harmonics = mode_orders.shape[0]
    columns = 2 * harmonics
    cols_loc = columns // pitch_count
    harm_loc = cols_loc // 2
    wavenumber = mode_orders[:, 0] * blade_counts[0] + mode_orders[:, 1] * blade_counts[1]
    analysis_scale = math.sqrt(2.0 / total_pitch)
    raw_local = pitch_table(wavenumber, pitch_at * pitch_location, pitch_location, total_pitch)
    local_table = (raw_local * analysis_scale).astype(jnp.bfloat16)
    flattened = planes.reshape(drawn_cases * fields * rad_loc, pitch_location)
    coefficients = lax.psum_scatter(
        lax.dot_general(
            local_table, flattened, (((0,), (1,)), ((), ())), preferred_element_type=jnp.float32
        ),
        "pitch",
        scatter_dimension=0,
        tiled=True,
    ).reshape(cols_loc, drawn_cases, fields, rad_loc)
    onsite_signal_trace = lax.dynamic_slice_in_dim(wavenumber, pitch_at * harm_loc, harm_loc)
    discrete_moments = cascade_index_map * drawn_cases + jnp.arange(drawn_cases, dtype=jnp.int32)
    vane_passing_interval = row_count * drawn_cases * blade_counts[0]
    angular_offsets = jnp.mod(
        onsite_signal_trace[:, None] * discrete_moments[None, :], vane_passing_interval
    )
    angles = (
        2.0
        * math.pi
        * angular_offsets.astype(jnp.float32)
        / vane_passing_interval.astype(jnp.float32)
    )
    cosine = jnp.cos(angles)[:, :, None, None]
    sine_part = jnp.sin(angles)[:, :, None, None]
    paired = coefficients.reshape(harm_loc, 2, drawn_cases, fields, rad_loc)
    cos_part = paired[:, 0]
    sin_part = paired[:, 1]
    rotated = jnp.stack(
        [cos_part * cosine - sin_part * sine_part, cos_part * sine_part + sin_part * cosine], axis=1
    )
    rotated = rotated.reshape(cols_loc, drawn_cases, fields, rad_loc).astype(jnp.bfloat16)
    radial_rows = span_at * rad_loc + jnp.arange(rad_loc, dtype=jnp.int32)
    in_band = (radial_rows[:, None] >= band_start[None, :]) & (
        radial_rows[:, None] < band_start[None, :] + BAND
    )
    banded = jnp.where(in_band, remap_weight, jnp.zeros_like(remap_weight))
    shift_by = row_count // 2
    partial_sums = lax.dot_general(
        rotated, banded, (((3,), (0,)), ((), ())), preferred_element_type=jnp.float32
    )
    remapped = passed_along(
        lax.psum_scatter(partial_sums, "span", scatter_dimension=3, tiled=True).astype(
            jnp.bfloat16
        ),
        "row",
        shift_by,
    )
    synth_table = (raw_local * (1.0 / math.sqrt(harmonics))).astype(jnp.bfloat16).T
    rs_loc = remapped.shape[3]
    shard_piece = lax.all_gather(remapped, "pitch", axis=0, tiled=True)
    number = shard_piece.shape[0]
    flattened_portion = shard_piece.reshape(number, drawn_cases * fields * rs_loc)
    summed = lax.dot_general(
        flattened_portion, synth_table, (((0,), (0,)), ((), ())), preferred_element_type=jnp.float32
    )
    return summed.reshape(1, drawn_cases, fields, rs_loc, pitch_location).astype(jnp.bfloat16)


def solution(mesh):
    placed = (P("row", None, None, "span", "pitch"), P("span", None), P(), P(), P())
    return jax.shard_map(
        body,
        mesh=mesh,
        in_specs=placed,
        out_specs=P("row", None, None, "span", "pitch"),
        check_vma=False,
    )
```

profile of v0, /device:TPU:2, one launch (start us, length us, event | category | flops | bytes accessed | tf_op | source)
XLA Modules:
  0.0 492.3 jit_solution(4572299544575242349)
XLA Ops:
  6.5 1.4 fusion.18
  7.9 2.0 fusion.24
  10.0 0.2 fusion.11
  10.3 2.0 fusion.19
  13.1 1.3 dynamic-slice.1
  15.1 1.3 multiply_add_fusion
  16.3 0.1 dynamic-slice_bitcast_fusion
  16.4 0.2 fusion.17
  16.7 276.1 %all-reduce.3.cloned.1.call-done = f32[128,5120]{1,0:T(8,128)} async-done(((f32[128,5120]{1,0:T(8,128)}), f32[128,5120]{1,0:T(8,128)}) %all-reduce.3.cloned.1.call-update) | async-done | bytes 2621456
  292.8 0.9 constant_dynamic-slice_fusion
  293.7 0.1 reshape_reshape.3
  293.8 0.1 subtract_convert_fusion
  293.9 0.5 fusion.3
  294.4 4.2 copy.20
  298.6 6.7 %reshape.252 = f32[896,40]{1,0:T(8,128)} reshape(f32[896,4,2,5]{3,2,1,0:T(2,128)} %bitcast.34) | data formatting | bytes 286720
  305.4 25.0 %reduce-scatter.4.cloned.1.call-done = f32[448,40]{1,0:T(8,128)} async-done(((f32[896,40]{1,0:T(8,128)}), f32[448,40]{1,0:T(8,128)}) %reduce-scatter.4.cloned.1.call-update) | async-done | bytes 71696
  330.4 1.5 reshape.253
  331.9 1.3 copy.21
  333.2 3.9 collective-permute-start
  337.0 3.8 collective-permute-done
  340.8 0.7 copy.13
  341.6 139.3 %all-gather.2.cloned.1.call-done = bf16[128,2,5,448]{3,1,2,0:T(2,128)(2,1)} async-done(((bf16[4,2,5,448]{3,1,2,0:T(2,128)(2,1)}), bf16[128,2,5,448]{3,1,2,0:T(2,128)(2,1)}) %all-gather.2.cloned.1.call-update) | async-done | bytes 1146896 | tf_op jit(solution)/shard_map/all_gather | solution.py:93
  480.9 3.5 copy.14
  484.4 1.4 fusion
  (22 shorter events, 0.3 us)
Async XLA Ops:
  6.5 3.7 copy-start
  6.5 286.2 %all-reduce.3.cloned.1.call-start = ((), (), s32[]{:S(2)}) async-start(), calls=%async_computation.3 | async-start | bytes 5242880
  12.3 2.8 copy-start.2
  12.3 4.4 copy-start.1
  12.3 281.6 %copy-start.3 = (bf16[512,896]{1,0:T(8,128)(2,1)S(1)}, bf16[512,896]{1,0:T(8,128)(2,1)}, u32[]{:S(2)}) copy-start(bf16[512,896]{1,0:T(8,128)(2,1)} %param.6) | copy-start | bytes 2752516
  12.3 318.0 %reduce-scatter.4.cloned.1.call-start = ((), (), s32[]{:S(2)}) async-start(), calls=%async_computation.2 | async-start | bytes 688128
  305.3 175.6 %all-gather.2.cloned.1.call-start = ((), (), s32[]{:S(2)}) async-start(), calls=%async_computation.1 | async-start | bytes 1351680 | tf_op jit(solution)/shard_map/all_gather | solution.py:93
  333.2 7.7 %collective-permute-start = (bf16[4,2,5,448]{3,2,1,0:T(8,128)(2,1)S(1)}, bf16[4,2,5,448]{3,2,1,0:T(8,128)(2,1)S(1)}, u32[]{:S(2)}, u32[]{:S(2)}) collective-permute-start(bf16[4,2,5,448]{3,2,1,0:T(8,128)(2,1)S(1)} %copy.21), channel_id=1, source_target_pairs={{0,512},{64,576},{128,640},{192,704},{256,768},{320,832},{384,896}... | collective-permute-start | bytes 107528 | tf_op jit(solution)/shard_map/ppermute | solution.py:14
Sparse Core Ops, SparseCore 0:
  12.4 280.3 all-reduce.2
  305.5 24.8 reduce-scatter.3
  341.6 139.2 all-gather.1
where the time goes:
time: 493 us; the launch traced here: 492 us
  waiting for transfers between devices  444 us (90%)
  local copies, waits for them, and re-layouts  21.6 us (4%)
  between operations  14.6 us (3%)
    unnamed x5, waiting for transfers between devices  301 us
    all_gather x1, waiting for transfers between devices, body(): shard_piece = lax.all_gather(remapped, 'pitch', axis=0, tiled=True)  139 us
    unnamed x14, local copies, waits for them, and re-layouts  15.9 us
  transfers between devices with their start and end apart: 4, of which 4 were waited for; matrix products, arithmetic and copies ran while one was open for 1% of the time, Pallas kernels for 0%

commit v1 on v0

v1 whole, which is shorter than its diff:
```python
import functools
import math

import jax
import jax.numpy as jnp
from jax import lax
from jax.experimental import pallas as pl
from jax.experimental.pallas import tpu as pltpu
from jax.sharding import PartitionSpec as P

BAND = 192
MESH = pl.DeviceIdType.MESH
F32 = jnp.float32
BF16 = jnp.bfloat16


def nt_dot(a, b):
    return lax.dot_general(a, b, (((1,), (1,)), ((), ())), preferred_element_type=F32)


def nn_dot(a, b):
    return lax.dot_general(a, b, (((1,), (0,)), ((), ())), preferred_element_type=F32)


def kernel(
    n, rows_n, chunk, subs, halo, half,
    x_ref, own_ref, cross_ref, ana_ref, syn_ref, rot_ref, out_ref,
    part, xsend, xrecv, sb_r, rb_r, sb_l, rb_l, fin, gath, outv,
    s_sr, s_rr, s_sl, s_rl, s_xs, s_xr, s_hs, s_hr, a_sr, a_rr, a_sl, a_rl, s_out,
):
    planes, rad, _ = x_ref.shape
    srows = own_ref.shape[0]
    width = cross_ref.shape[1]
    sub = chunk // subs
    z = lax.axis_index("pitch")
    g = lax.axis_index("row")
    h = lax.axis_index("span")
    right = lax.rem(z + 1, n)
    left = lax.rem(z + n - 1, n)
    other = 1 - h
    partner = lax.rem(g + rows_n // 2, rows_n)
    hops_r = n // 2
    hops_l = n - 1 - hops_r

    barrier = pltpu.get_barrier_semaphore()
    for where in ({"pitch": left}, {"pitch": right}, {"span": other}, {"row": partner}):
        pl.semaphore_signal(barrier, inc=1, device_id=where, device_id_type=MESH)

    cols0 = (rad - width) * (1 - h)
    def cross_plane(k, c):
        xk = x_ref[k, pl.ds(pl.multiple_of(cols0, 128), width), :]
        xsend[k] = nn_dot(cross_ref[...], xk).astype(BF16)
        return c
    lax.fori_loop(0, planes, cross_plane, 0)

    pl.semaphore_wait(barrier, 4)
    xcopy = pltpu.make_async_remote_copy(
        src_ref=xsend, dst_ref=xrecv, send_sem=s_xs, recv_sem=s_xr,
        device_id={"span": other}, device_id_type=MESH)
    xcopy.start()

    ana = ana_ref[...]
    def own_plane(k, c):
        mk = nn_dot(own_ref[...], x_ref[k]).astype(BF16)
        part[pl.ds(pl.multiple_of(k * srows, 16), srows), :] = nt_dot(mk, ana)
        return c
    lax.fori_loop(0, planes, own_plane, 0)
    tail = part.shape[0] - planes * srows
    if tail:
        part[planes * srows:, :] = jnp.zeros((tail, part.shape[1]), F32)
    xcopy.wait_recv()
    b0 = (srows - halo) * (1 - h)
    def add_plane(k, c):
        at = pl.ds(pl.multiple_of(k * srows + b0, 16), halo)
        part[at, :] = part[at, :] + nt_dot(xrecv[k], ana)
        return c
    lax.fori_loop(0, planes, add_plane, 0)

    def rows_of(c, j):
        return pl.ds(pl.multiple_of(c * chunk + j * sub, 16), sub)

    def send_r(s, j):
        return pltpu.make_async_remote_copy(
            src_ref=sb_r.at[s, j], dst_ref=rb_r.at[s, j], send_sem=s_sr.at[s, j], recv_sem=s_rr.at[s, j],
            device_id={"pitch": right}, device_id_type=MESH)

    def send_l(s, j):
        return pltpu.make_async_remote_copy(
            src_ref=sb_l.at[s, j], dst_ref=rb_l.at[s, j], send_sem=s_sl.at[s, j], recv_sem=s_rl.at[s, j],
            device_id={"pitch": left}, device_id_type=MESH)

    def chunk_r(s):
        return lax.rem(z + hops_r - s + n, n)

    def chunk_l(s):
        return lax.rem(z - hops_l + s + n, n)

    for j in range(subs):
        sb_r[0, j] = part[rows_of(chunk_r(0), j), :].astype(BF16)
        send_r(0, j).start()
        sb_l[0, j] = part[rows_of(chunk_l(0), j), :].astype(BF16)
        send_l(0, j).start()

    def step(s, c):
        for j in range(subs):
            send_r(s - 1, j).wait_recv()
            sb_r[s, j] = (part[rows_of(chunk_r(s), j), :] + rb_r[s - 1, j].astype(F32)).astype(BF16)
            send_r(s, j).start()
            send_l(s - 1, j).wait_recv()
            sb_l[s, j] = (part[rows_of(chunk_l(s), j), :] + rb_l[s - 1, j].astype(F32)).astype(BF16)
            send_l(s, j).start()
        return c
    lax.fori_loop(1, hops_l, step, 0)
    for s in range(hops_l, hops_r):
        for j in range(subs):
            send_r(s - 1, j).wait_recv()
            sb_r[s, j] = (part[rows_of(chunk_r(s), j), :] + rb_r[s - 1, j].astype(F32)).astype(BF16)
            send_r(s, j).start()

    cut = half * srows

    def hop(j):
        return pltpu.make_async_remote_copy(
            src_ref=fin.at[j], dst_ref=gath.at[z, j], send_sem=s_hs.at[j], recv_sem=s_hr.at[j],
            device_id={"row": partner}, device_id_type=MESH)

    for j in range(subs):
        send_l(hops_l - 1, j).wait_recv()
        total = part[rows_of(z, j), :] + rb_l[hops_l - 1, j].astype(F32)
        send_r(hops_r - 1, j).wait_recv()
        total = total + rb_r[hops_r - 1, j].astype(F32)
        at = z * chunk + j * sub + lax.broadcasted_iota(jnp.int32, total.shape, 0)
        first = at < cut
        cosine = jnp.where(first, rot_ref[0:1, :], rot_ref[1:2, :])
        sine = jnp.where(first, rot_ref[2:3, :], rot_ref[3:4, :])
        swapped = pltpu.roll(total, total.shape[1] // 2, 1)
        fin[j] = (total * cosine + swapped * sine).astype(BF16)
        hop(j).start()

    def fwd_r(s, j):
        at = gath.at[lax.rem(z - s + n, n), j]
        return pltpu.make_async_remote_copy(
            src_ref=at, dst_ref=at, send_sem=a_sr.at[s, j], recv_sem=a_rr.at[s, j],
            device_id={"pitch": right}, device_id_type=MESH)

    def fwd_l(s, j):
        at = gath.at[lax.rem(z + s, n), j]
        return pltpu.make_async_remote_copy(
            src_ref=at, dst_ref=at, send_sem=a_sl.at[s, j], recv_sem=a_rl.at[s, j],
            device_id={"pitch": left}, device_id_type=MESH)

    def recv_r(s, j):
        at = gath.at[lax.rem(z - s - 1 + n, n), j]
        return pltpu.make_async_remote_copy(
            src_ref=at, dst_ref=at, send_sem=a_sr.at[s, j], recv_sem=a_rr.at[s, j],
            device_id={"pitch": right}, device_id_type=MESH)

    def recv_l(s, j):
        at = gath.at[lax.rem(z + s + 1, n), j]
        return pltpu.make_async_remote_copy(
            src_ref=at, dst_ref=at, send_sem=a_sl.at[s, j], recv_sem=a_rl.at[s, j],
            device_id={"pitch": left}, device_id_type=MESH)

    syn = syn_ref[...]

    def emit(c, j):
        outv[rows_of(c, j), :] = nn_dot(gath[c, j], syn).astype(BF16)

    for j in range(subs):
        hop(j).wait_recv()
        fwd_r(0, j).start()
        fwd_l(0, j).start()
    for j in range(subs):
        emit(z, j)

    def ag_step(s, c):
        for j in range(subs):
            recv_r(s - 1, j).wait_recv()
            fwd_r(s, j).start()
            recv_l(s - 1, j).wait_recv()
            fwd_l(s, j).start()
        for j in range(subs):
            emit(lax.rem(z - s + n, n), j)
            emit(lax.rem(z + s, n), j)
        return c
    lax.fori_loop(1, hops_l, ag_step, 0)
    for s in range(hops_l, hops_r):
        for j in range(subs):
            recv_r(s - 1, j).wait_recv()
            fwd_r(s, j).start()
        for j in range(subs):
            emit(lax.rem(z - s + n, n), j)
    for j in range(subs):
        recv_l(hops_l - 1, j).wait_recv()
        emit(lax.rem(z + hops_l, n), j)
    for j in range(subs):
        recv_r(hops_r - 1, j).wait_recv()
        emit(lax.rem(z - hops_r + n, n), j)

    done = pltpu.make_async_copy(outv.at[pl.ds(0, planes * srows)], out_ref, s_out)
    done.start()

    xcopy.wait_send()
    for j in range(subs):
        hop(j).wait_send()

    def drain_r(s, c):
        for j in range(subs):
            send_r(s, j).wait_send()
            fwd_r(s, j).wait_send()
        return c
    lax.fori_loop(0, hops_r, drain_r, 0)

    def drain_l(s, c):
        for j in range(subs):
            send_l(s, j).wait_send()
            fwd_l(s, j).wait_send()
        return c
    lax.fori_loop(0, hops_l, drain_l, 0)
    done.wait()


def body(outlet, remap_weight, band_start, blade_counts, mode_orders):
    row_count = lax.axis_size("row")
    n = lax.axis_size("pitch")
    g = lax.axis_index("row")
    z = lax.axis_index("pitch")
    h = lax.axis_index("span")
    planes = outlet[0]
    inst, fields, rad, pitch = planes.shape
    total_pitch = pitch * n
    harm = mode_orders.shape[0]
    cols = 2 * harm
    stator = remap_weight.shape[1]
    srows = stator // 2
    nplanes = inst * fields
    wave = mode_orders[:, 0] * blade_counts[0] + mode_orders[:, 1] * blade_counts[1]

    place = z * pitch + jnp.arange(pitch, dtype=jnp.int32)
    q = jnp.mod(place[None, :] * wave[:, None], total_pitch)
    ang = 2.0 * math.pi / total_pitch * q.astype(F32)
    table = jnp.concatenate([jnp.cos(ang), jnp.sin(ang)], axis=0)
    ana = (table * math.sqrt(2.0 / total_pitch)).astype(BF16)
    syn = (table * (1.0 / math.sqrt(harm))).astype(BF16)

    moments = g * inst + jnp.arange(inst, dtype=jnp.int32)
    period = row_count * inst * blade_counts[0]
    turn = jnp.mod(wave[None, :] * moments[:, None], period)
    theta = 2.0 * math.pi * turn.astype(F32) / period.astype(F32)
    co, si = jnp.cos(theta), jnp.sin(theta)
    rot = jnp.concatenate(
        [jnp.concatenate([co, co], 1), jnp.concatenate([-si, si], 1), jnp.zeros((8 - 2 * inst, cols), F32)], 0)

    rows = h * rad + jnp.arange(rad, dtype=jnp.int32)
    inb = (rows[:, None] >= band_start[None, :]) & (rows[:, None] < band_start[None, :] + BAND)
    banded = jnp.where(inb, remap_weight, jnp.zeros_like(remap_weight)).T
    halo, width = 112, 128
    own = lax.dynamic_slice_in_dim(banded, h * srows, srows, 0)
    cross = lax.dynamic_slice(banded, (srows - halo * h, (rad - width) * (1 - h)), (halo, width))

    nrows = nplanes * srows
    chunk = -(-nrows // (n * 16)) * 16
    subs = 3 if chunk % 48 == 0 else (2 if chunk % 32 == 0 else 1)
    sub = chunk // subs
    hr, hl = n // 2, n - 1 - n // 2
    vm = pl.BlockSpec(memory_space=pltpu.VMEM)
    out = pl.pallas_call(
        functools.partial(kernel, n, row_count, chunk, subs, halo, fields),
        out_shape=jax.ShapeDtypeStruct((nrows, pitch), BF16),
        in_specs=[vm] * 6,
        out_specs=pl.BlockSpec(memory_space=pl.ANY),
        scratch_shapes=[
            pltpu.VMEM((n * chunk, cols), F32),
            pltpu.VMEM((nplanes, halo, pitch), BF16),
            pltpu.VMEM((nplanes, halo, pitch), BF16),
            pltpu.VMEM((hr, subs, sub, cols), BF16),
            pltpu.VMEM((hr, subs, sub, cols), BF16),
            pltpu.VMEM((hl, subs, sub, cols), BF16),
            pltpu.VMEM((hl, subs, sub, cols), BF16),
            pltpu.VMEM((subs, sub, cols), BF16),
            pltpu.VMEM((n, subs, sub, cols), BF16),
            pltpu.VMEM((n * chunk, pitch), BF16),
            pltpu.SemaphoreType.DMA((hr, subs)),
            pltpu.SemaphoreType.DMA((hr, subs)),
            pltpu.SemaphoreType.DMA((hl, subs)),
            pltpu.SemaphoreType.DMA((hl, subs)),
            pltpu.SemaphoreType.DMA,
            pltpu.SemaphoreType.DMA,
            pltpu.SemaphoreType.DMA((subs,)),
            pltpu.SemaphoreType.DMA((subs,)),
            pltpu.SemaphoreType.DMA((hr, subs)),
            pltpu.SemaphoreType.DMA((hr, subs)),
            pltpu.SemaphoreType.DMA((hl, subs)),
            pltpu.SemaphoreType.DMA((hl, subs)),
            pltpu.SemaphoreType.DMA,
        ],
        compiler_params=pltpu.CompilerParams(
            collective_id=0, has_side_effects=True, vmem_limit_bytes=40 * 1024 * 1024),
    )(planes.reshape(nplanes, rad, pitch), own, cross, ana, syn, rot)
    return out.reshape(1, inst, fields, srows, pitch)


def solution(mesh):
    placed = (P("row", None, None, "span", "pitch"), P("span", None), P(), P(), P())
    return jax.shard_map(
        body, mesh=mesh, in_specs=placed,
        out_specs=P("row", None, None, "span", "pitch"), check_vma=False)
```

time: 493 us -> 141 us (0.29)
  the two profiles are of different devices: /device:TPU:2 before, /device:TPU:8 now
where the time goes in v1:
time: 141 us
  Pallas kernels  132 us (94%)
  local copies, waits for them, and re-layouts  4.74 us (3%)
  other arithmetic  3.6 us (3%)
    pallas_call x1, Pallas kernels, body(): pl.pallas_call(functools.partial(kernel, n, row_count, chunk, subs, halo,...  132 us
    unnamed x6, local copies, waits for them, and re-layouts  3.3 us

profile of v1, /device:TPU:8, one launch (start us, length us, event | category | flops | bytes accessed | tf_op | source)
XLA Modules:
  0.0 141.1 jit_solution(14033009969386676421)
XLA Ops:
  0.0 0.0 copy-start.1
  0.0 0.1 pad.4.clone
  0.1 1.3 fusion.12
  2.1 2.0 %add_bitcast_fusion = s32[64]{0:T(128)S(1)} fusion(s32[64,2]{0,1:T(2,128)} %param.9, s32[]{:T(128)} %bitcast.4, s32[]{:T(128)} %bitcast.3), kind=kLoop, calls=%fused_computation.24 | loop fusion | flops 192 | bytes 776 | tf_op jit(solution)/shard_map/mul | solution.py:240
  4.0 0.2 fusion.10
  4.3 0.1 maximum_maximum_fusion.rot_ref
  4.3 0.7 broadcast_add_fusion
  5.0 0.2 fusion.4
  5.3 1.5 %copy.6 = bf16[512,896]{0,1:T(8,128)(2,1)S(1)} copy(bf16[512,896]{1,0:T(8,128)(2,1)} %param.6) | data formatting | bytes 1835008 | tf_op args[1]
  6.7 0.0 copy-done.1
  6.8 0.0 copy-start
  6.8 0.4 and_select_fusion
  7.2 0.8 copy-done
  8.1 132.0 %shard_map.55 = bf16[4480,128]{1,0:T(8,128)(2,1)S(1)} custom-call(bf16[10,512,128]{2,1,0:T(8,128)(2,1)S(1)} %bitcast.11, bf16[448,512]{1,0:T(8,128)(2,1)S(1)} %dynamic-slice_bitcast_fusion.own_ref, bf16[112,128]{1,0:T(8,128)(2,1)S(1)} %dynamic-slice_bitcast_fusion.1.cross_ref, bf16[128,128]{1,0:T(8,128)(2,1)S(1)} %get-tuple-element.8.ana_ref, ...), custom_call_target="tpu_custom_call" | custom-call | tf_op jit(solution)/shard_map/pallas_call | solution.py:267
  140.1 1.0 copy.8
  (7 shorter events, 0.1 us)
Async XLA Ops:
  0.0 6.7 %copy-start.1 = (s32[896]{0:T(1024)S(1)}, s32[896]{0:T(1024)}, u32[]{:S(2)}) copy-start(s32[896]{0:T(1024)} %param.7) | copy-start | bytes 10756
  6.8 1.3 copy-start

commit v2 on v1

v2 whole, which is shorter than its diff:
```python
import functools
import math

import jax
import jax.numpy as jnp
from jax import lax
from jax.experimental import pallas as pl
from jax.experimental.pallas import tpu as pltpu
from jax.sharding import PartitionSpec as P

BAND = 192
MESH = pl.DeviceIdType.MESH
F32 = jnp.float32
BF16 = jnp.bfloat16


def nt_dot(a, b):
    return lax.dot_general(a, b, (((1,), (1,)), ((), ())), preferred_element_type=F32)


def nn_dot(a, b):
    return lax.dot_general(a, b, (((1,), (0,)), ((), ())), preferred_element_type=F32)


def kernel(
    n, rows_n, chunk, halo, half,
    x_ref, own_ref, cross_ref, ana_ref, syn_ref, rot_ref, out_ref,
    part, xsend, xrecv, sb_r, rb_r, sb_l, rb_l, sums, from_roots, gath,
    s_sr, s_rr, s_sl, s_rl, s_xs, s_xr, e_s, e_r, g_s, g_r, a_sr, a_rr, a_sl, a_rl,
):
    planes, rad, _ = x_ref.shape
    srows = own_ref.shape[0]
    width = cross_ref.shape[1]
    reach = (n - 2) // 6
    far = 2 * reach + 1
    z = lax.axis_index("pitch")
    g = lax.axis_index("row")
    h = lax.axis_index("span")
    other = 1 - h
    partner = lax.rem(g + rows_n // 2, rows_n)

    def at(d):
        return lax.rem(z + (d + n), n)

    right, left = at(1), at(-1)
    offsets = (far, -far, 0)

    barrier = pltpu.get_barrier_semaphore()
    peers = [{"pitch": left}, {"pitch": right}, {"span": other}]
    peers += [{"pitch": at(far)}, {"pitch": at(-far)}]
    peers += [{"row": partner, "pitch": at(d)} for d in offsets]
    for where in peers:
        pl.semaphore_signal(barrier, inc=1, device_id=where, device_id_type=MESH)

    cols0 = (rad - width) * (1 - h)

    def cross_plane(k, c):
        xk = x_ref[k, pl.ds(pl.multiple_of(cols0, 128), width), :]
        xsend[k] = nn_dot(cross_ref[...], xk).astype(BF16)
        return c

    lax.fori_loop(0, planes, cross_plane, 0)

    pl.semaphore_wait(barrier, len(peers))

    def remote(src, dst, send, recv, where):
        return pltpu.make_async_remote_copy(
            src_ref=src, dst_ref=dst, send_sem=send, recv_sem=recv, device_id=where, device_id_type=MESH
        )

    xcopy = remote(xsend, xrecv, s_xs, s_xr, {"span": other})
    xcopy.start()

    ana = ana_ref[...]

    def own_plane(k, c):
        mk = nn_dot(own_ref[...], x_ref[k]).astype(BF16)
        part[pl.ds(pl.multiple_of(k * srows, 16), srows), :] = nt_dot(mk, ana)
        return c

    lax.fori_loop(0, planes, own_plane, 0)
    tail = part.shape[0] - planes * srows
    if tail:
        part[planes * srows :, :] = jnp.zeros((tail, part.shape[1]), F32)
    xcopy.wait_recv()
    b0 = (srows - halo) * (1 - h)

    def add_plane(k, c):
        rows = pl.ds(pl.multiple_of(k * srows + b0, 16), halo)
        part[rows, :] = part[rows, :] + nt_dot(xrecv[k], ana)
        return c

    lax.fori_loop(0, planes, add_plane, 0)

    def rows_of(c):
        return pl.ds(pl.multiple_of(c * chunk, 16), chunk)

    def send_r(s, k):
        return remote(sb_r.at[s, k], rb_r.at[s, k], s_sr.at[s, k], s_rr.at[s, k], {"pitch": right})

    def send_l(s, k):
        return remote(sb_l.at[s, k], rb_l.at[s, k], s_sl.at[s, k], s_rl.at[s, k], {"pitch": left})

    def first_r(k):
        return 1 if k == 1 else 0

    for s in range(reach):
        for k, off in enumerate(offsets):
            if s >= first_r(k):
                value = part[rows_of(at(reach - s - off)), :]
                if s > first_r(k):
                    send_r(s - 1, k).wait_recv()
                    value = value + rb_r[s - 1, k].astype(F32)
                sb_r[s, k] = value.astype(BF16)
                send_r(s, k).start()
            value = part[rows_of(at(s - reach - off)), :]
            if s > 0:
                send_l(s - 1, k).wait_recv()
                value = value + rb_l[s - 1, k].astype(F32)
            sb_l[s, k] = value.astype(BF16)
            send_l(s, k).start()

    def to_owner(k):
        where = {"row": partner, "pitch": at(-offsets[k])}
        return remote(sums.at[k], from_roots.at[k], e_s.at[k], e_r.at[k], where)

    for k, off in enumerate(offsets):
        value = part[rows_of(at(-off)), :]
        send_l(reach - 1, k).wait_recv()
        value = value + rb_l[reach - 1, k].astype(F32)
        if reach - 1 >= first_r(k):
            send_r(reach - 1, k).wait_recv()
            value = value + rb_r[reach - 1, k].astype(F32)
        sums[k] = value.astype(BF16)
        to_owner(k).start()

    for k in range(3):
        to_owner(k).wait_recv()
    total = from_roots[2].astype(F32) + from_roots[0].astype(F32) + from_roots[1].astype(F32)
    place = z * chunk + lax.broadcasted_iota(jnp.int32, total.shape, 0)
    first = place < half * srows
    cosine = jnp.where(first, rot_ref[0:1, :], rot_ref[1:2, :])
    sine = jnp.where(first, rot_ref[2:3, :], rot_ref[3:4, :])
    swapped = pltpu.roll(total, total.shape[1] // 2, 1)
    gath[z] = (total * cosine + swapped * sine).astype(BF16)

    def to_root(k, incoming=False):
        c = gath.at[at(-offsets[k])] if incoming else gath.at[z]
        return remote(c, c, g_s.at[k], g_r.at[k], {"pitch": at(offsets[k])})

    def fwd_r(s, k, incoming=False):
        c = gath.at[at(-s - (1 if incoming else 0) - offsets[k])]
        return remote(c, c, a_sr.at[s, k], a_rr.at[s, k], {"pitch": right})

    def fwd_l(s, k, incoming=False):
        c = gath.at[at(s + (1 if incoming else 0) - offsets[k])]
        return remote(c, c, a_sl.at[s, k], a_rl.at[s, k], {"pitch": left})

    def last_l(k):
        return reach - 2 if k == 1 else reach - 1

    syn = syn_ref[...]

    def emit(c):
        out_ref[rows_of(c), :] = nn_dot(gath[c], syn).astype(BF16)

    to_root(0).start()
    to_root(1).start()
    fwd_r(0, 2).start()
    fwd_l(0, 2).start()
    emit(z)

    def take(k, s):
        ready = []
        if s == 0:
            to_root(k, True).wait_recv()
            fwd_r(0, k).start()
            if last_l(k) >= 0:
                fwd_l(0, k).start()
            ready.append(at(-offsets[k]))
        else:
            fwd_r(s - 1, k, True).wait_recv()
            if s < reach:
                fwd_r(s, k).start()
            ready.append(at(-s - offsets[k]))
            if s - 1 <= last_l(k):
                fwd_l(s - 1, k, True).wait_recv()
                if s <= last_l(k):
                    fwd_l(s, k).start()
                ready.append(at(s - offsets[k]))
        return ready

    lag = min(3, reach)
    for t in range(1, reach + lag + 1):
        ready = []
        if t <= reach:
            ready += take(2, t)
        if t >= lag:
            ready += take(0, t - lag)
            ready += take(1, t - lag)
        for c in ready:
            emit(c)

    xcopy.wait_send()
    for k in range(3):
        to_owner(k).wait_send()
        if k < 2:
            to_root(k).wait_send()
        for s in range(reach):
            if s >= first_r(k):
                send_r(s, k).wait_send()
            send_l(s, k).wait_send()
            fwd_r(s, k).wait_send()
            if s <= last_l(k):
                fwd_l(s, k).wait_send()


def body(outlet, remap_weight, band_start, blade_counts, mode_orders):
    row_count = lax.axis_size("row")
    n = lax.axis_size("pitch")
    g = lax.axis_index("row")
    z = lax.axis_index("pitch")
    h = lax.axis_index("span")
    planes = outlet[0]
    inst, fields, rad, pitch = planes.shape
    total_pitch = pitch * n
    harm = mode_orders.shape[0]
    cols = 2 * harm
    stator = remap_weight.shape[1]
    srows = stator // 2
    nplanes = inst * fields
    wave = mode_orders[:, 0] * blade_counts[0] + mode_orders[:, 1] * blade_counts[1]

    place = z * pitch + jnp.arange(pitch, dtype=jnp.int32)
    q = jnp.mod(place[None, :] * wave[:, None], total_pitch)
    ang = 2.0 * math.pi / total_pitch * q.astype(F32)
    table = jnp.concatenate([jnp.cos(ang), jnp.sin(ang)], axis=0)
    ana = (table * math.sqrt(2.0 / total_pitch)).astype(BF16)
    syn = (table * (1.0 / math.sqrt(harm))).astype(BF16)

    moments = lax.rem(g + row_count // 2, row_count) * inst + jnp.arange(inst, dtype=jnp.int32)
    period = row_count * inst * blade_counts[0]
    turn = jnp.mod(wave[None, :] * moments[:, None], period)
    theta = 2.0 * math.pi * turn.astype(F32) / period.astype(F32)
    co, si = jnp.cos(theta), jnp.sin(theta)
    rot = jnp.concatenate(
        [jnp.concatenate([co, co], 1), jnp.concatenate([-si, si], 1), jnp.zeros((8 - 2 * inst, cols), F32)], 0)

    rows = h * rad + jnp.arange(rad, dtype=jnp.int32)
    inb = (rows[:, None] >= band_start[None, :]) & (rows[:, None] < band_start[None, :] + BAND)
    banded = jnp.where(inb, remap_weight, jnp.zeros_like(remap_weight)).T
    halo, width = 112, 128
    own = lax.dynamic_slice_in_dim(banded, h * srows, srows, 0)
    cross = lax.dynamic_slice(banded, (srows - halo * h, (rad - width) * (1 - h)), (halo, width))

    nrows = nplanes * srows
    chunk = -(-nrows // (n * 16)) * 16
    reach = (n - 2) // 6
    sem = pltpu.SemaphoreType.DMA
    vm = pl.BlockSpec(memory_space=pltpu.VMEM)
    out = pl.pallas_call(
        functools.partial(kernel, n, row_count, chunk, halo, fields),
        out_shape=jax.ShapeDtypeStruct((n * chunk, pitch), BF16),
        in_specs=[vm] * 6,
        out_specs=vm,
        scratch_shapes=[
            pltpu.VMEM((n * chunk, cols), F32),
            pltpu.VMEM((nplanes, halo, pitch), BF16),
            pltpu.VMEM((nplanes, halo, pitch), BF16),
            pltpu.VMEM((reach, 3, chunk, cols), BF16),
            pltpu.VMEM((reach, 3, chunk, cols), BF16),
            pltpu.VMEM((reach, 3, chunk, cols), BF16),
            pltpu.VMEM((reach, 3, chunk, cols), BF16),
            pltpu.VMEM((3, chunk, cols), BF16),
            pltpu.VMEM((3, chunk, cols), BF16),
            pltpu.VMEM((n, chunk, cols), BF16),
            sem((reach, 3)),
            sem((reach, 3)),
            sem((reach, 3)),
            sem((reach, 3)),
            sem,
            sem,
            sem((3,)),
            sem((3,)),
            sem((2,)),
            sem((2,)),
            sem((reach, 3)),
            sem((reach, 3)),
            sem((reach, 3)),
            sem((reach, 3)),
        ],
        compiler_params=pltpu.CompilerParams(
            collective_id=0, has_side_effects=True, vmem_limit_bytes=40 * 1024 * 1024
        ),
    )(planes.reshape(nplanes, rad, pitch), own, cross, ana, syn, rot)
    return out[:nrows].reshape(1, inst, fields, srows, pitch)


def solution(mesh):
    placed = (P("row", None, None, "span", "pitch"), P("span", None), P(), P(), P())
    return jax.shard_map(
        body, mesh=mesh, in_specs=placed,
        out_specs=P("row", None, None, "span", "pitch"), check_vma=False)
```

time: 141 us -> 112 us (0.79)
  Pallas kernels: 132 us -> 103 us
    pallas_call x1, Pallas kernels: 132 us -> 103 us  [body(): pl.pallas_call(functools.partial(kernel, n, row_count, chunk, halo, field...]
    unnamed x6 -> x5, local copies, waits for them, and re-layouts: 3.3 us -> 2.3 us
where the time goes in v2:
time: 112 us
  Pallas kernels  103 us (92%)
  local copies, waits for them, and re-layouts  4.81 us (4%)
  other arithmetic  3.6 us (3%)
    pallas_call x1, Pallas kernels, body(): pl.pallas_call(functools.partial(kernel, n, row_count, chunk, halo, field...  103 us
    unnamed x5, local copies, waits for them, and re-layouts  2.3 us

profile of v2, /device:TPU:8, one launch (start us, length us, event | category | flops | bytes accessed | tf_op | source)
XLA Modules:
  0.0 111.9 jit_solution(610653161172898834)
XLA Ops:
  0.0 0.0 copy-start.1
  0.0 0.1 pad.4.clone
  0.1 1.3 %fusion.12 = (s32[1]{0:T(128)}, s32[1]{0:T(128)}) fusion(s32[2]{0:T(128)} %param.8), kind=kLoop, calls=%fused_computation.29 | loop fusion | bytes 16 | tf_op jit(solution)/shard_map/slice | solution.py:232
  2.1 2.0 %add_bitcast_fusion = s32[64]{0:T(128)S(1)} fusion(s32[64,2]{0,1:T(2,128)} %param.9, s32[]{:T(128)} %bitcast.4, s32[]{:T(128)} %bitcast.3), kind=kLoop, calls=%fused_computation.24 | loop fusion | flops 192 | bytes 776 | tf_op jit(solution)/shard_map/mul | solution.py:235
  4.0 0.2 fusion.10
  4.3 0.1 maximum_maximum_fusion.rot_ref
  4.3 0.7 broadcast_add_fusion
  5.0 0.2 fusion.4
  5.3 1.5 %copy.6 = bf16[512,896]{0,1:T(8,128)(2,1)S(1)} copy(bf16[512,896]{1,0:T(8,128)(2,1)} %param.6) | data formatting | bytes 1835008 | tf_op args[1]
  6.7 0.0 copy-done.1
  6.8 0.0 copy-start
  6.8 0.4 and_select_fusion
  7.2 0.8 copy-done
  8.1 102.7 %shard_map.55 = bf16[4608,128]{1,0:T(8,128)(2,1)S(1)} custom-call(bf16[10,512,128]{2,1,0:T(8,128)(2,1)S(1)} %bitcast.10, bf16[448,512]{1,0:T(8,128)(2,1)S(1)} %dynamic-slice_bitcast_fusion.own_ref, bf16[112,128]{1,0:T(8,128)(2,1)S(1)} %dynamic-slice_bitcast_fusion.1.cross_ref, bf16[128,128]{1,0:T(8,128)(2,1)S(1)} %get-tuple-element.8.ana_ref, ...), custom_call_target="tpu_custom_call" | custom-call | tf_op jit(solution)/shard_map/pallas_call | solution.py:261
  110.8 1.1 slice.20
  (7 shorter events, 0.1 us)
Async XLA Ops:
  0.0 6.7 %copy-start.1 = (s32[896]{0:T(1024)S(1)}, s32[896]{0:T(1024)}, u32[]{:S(2)}) copy-start(s32[896]{0:T(1024)} %param.7) | copy-start | bytes 10756
  6.8 1.3 %copy-start = (bf16[1,2,5,512,128]{4,3,2,1,0:T(8,128)(2,1)S(1)}, bf16[1,2,5,512,128]{4,3,2,1,0:T(8,128)(2,1)}, u32[]{:S(2)}) copy-start(bf16[1,2,5,512,128]{4,3,2,1,0:T(8,128)(2,1)} %param.5) | copy-start | bytes 3932164

commit v3 on v2

v3 whole, which is shorter than its diff:
```python
import functools
import math

import jax
import jax.numpy as jnp
from jax import lax
from jax.experimental import pallas as pl
from jax.experimental.pallas import tpu as pltpu
from jax.sharding import PartitionSpec as P

BAND = 192
SUBS = 1
LAG = 2
MESH = pl.DeviceIdType.MESH
F32 = jnp.float32
BF16 = jnp.bfloat16


def nt_dot(a, b):
    return lax.dot_general(a, b, (((1,), (1,)), ((), ())), preferred_element_type=F32)


def nn_dot(a, b):
    return lax.dot_general(a, b, (((1,), (0,)), ((), ())), preferred_element_type=F32)


def wrapped(value, size):
    if size & (size - 1) == 0:
        return value & (size - 1)
    return jnp.mod(value, size)


def kernel(
    n, rows_n, chunk, subs, halo, half, srows,
    x_hbm, w_hbm, start_hbm, blade_hbm, order_hbm, out_hbm,
    x_ref, w_ref, start_ref, blade_ref, order_ref, out_ref, band_t, ana_ref, syn_ref, rot_ref,
    part, xsend, xrecv, sb_r, rb_r, sb_l, rb_l, sums, from_roots, gath,
    s_sr, s_rr, s_sl, s_rl, s_xs, s_xr, e_s, e_r, g_s, g_r, a_sr, a_rr, a_sl, a_rl, s_in, s_out, token,
):
    planes, rad, _ = x_ref.shape
    width = 128
    sub = chunk // subs
    reach = (n - 2) // 6
    far = 2 * reach + 1
    z = lax.axis_index("pitch")
    g = lax.axis_index("row")
    h = lax.axis_index("span")
    other = 1 - h
    partner = lax.rem(g + rows_n // 2, rows_n)

    def at(d):
        return lax.rem(z + (d + n), n)

    right, left = at(1), at(-1)
    offsets = (far, -far, 0)

    barrier = pltpu.get_barrier_semaphore()
    pace = (reach + 1) // 2
    ahead, behind = at(pace), at(-pace)
    peers = [{"pitch": left}, {"pitch": right}, {"span": other}, {"row": partner}]
    peers += [{"pitch": ahead}, {"pitch": behind}]
    for where in peers:
        pl.semaphore_signal(barrier, inc=1, device_id=where, device_id_type=MESH)

    x_in = pltpu.make_async_copy(x_hbm, x_ref, s_in.at[0])
    w_in = pltpu.make_async_copy(w_hbm, w_ref, s_in.at[1])
    start_in = pltpu.make_async_copy(start_hbm, start_ref, s_in.at[2])
    blade_in = pltpu.make_async_copy(blade_hbm, blade_ref, s_in.at[3])
    order_in = pltpu.make_async_copy(order_hbm, order_ref, s_in.at[4])
    blade_in.start()
    order_in.start()
    start_in.start()
    w_in.start()
    x_in.start()

    harm = order_ref.shape[1]
    blade_in.wait()
    order_in.wait()
    pitch = x_ref.shape[2]
    total_pitch = pitch * n
    wave_row = order_ref[0:1, :] * blade_ref[0] + order_ref[1:2, :] * blade_ref[1]
    wave = jnp.broadcast_to(wave_row.astype(F32), (128, harm)).T.astype(jnp.int32)
    spot = z * pitch + lax.broadcasted_iota(jnp.int32, (harm, pitch), 1)
    turns = wrapped(spot * wave, total_pitch)
    angle = 2.0 * math.pi / total_pitch * turns.astype(F32)
    both = jnp.concatenate([jnp.cos(angle), jnp.sin(angle)], axis=0)
    ana_ref[...] = (both * math.sqrt(2.0 / total_pitch)).astype(BF16)
    syn_ref[...] = (both * (1.0 / math.sqrt(harm))).astype(BF16)

    inst = planes // half
    moment = partner * inst + lax.broadcasted_iota(jnp.int32, (harm, 128), 1)
    steps = (wave * moment).astype(F32)
    period = (rows_n * inst * blade_ref[0]).astype(F32)
    left_over = steps - jnp.floor(steps / period) * period
    left_over = jnp.where(left_over < 0.0, left_over + period, left_over)
    left_over = jnp.where(left_over >= period, left_over - period, left_over)
    theta = 2.0 * math.pi * left_over / period
    cos_t, sin_t = jnp.cos(theta), jnp.sin(theta)
    rot_ref[0] = jnp.concatenate([cos_t, cos_t], axis=0).T
    rot_ref[1] = jnp.concatenate([-sin_t, sin_t], axis=0).T

    w_in.wait()
    start_in.wait()
    block = 128

    def band_rows(r, c):
        at_r = pl.ds(pl.multiple_of(r * block, block), block)
        rows = h * rad + r * block + lax.broadcasted_iota(jnp.int32, (block, w_ref.shape[1]), 0)
        begin = start_ref[...].reshape(1, w_ref.shape[1])
        inb = (rows >= begin) & (rows < begin + BAND)
        kept = jnp.where(inb, w_ref[at_r, :].astype(F32), 0.0)
        band_t[:, at_r] = kept.T.astype(BF16)
        return c

    lax.fori_loop(0, rad // block, band_rows, 0)
    x_in.wait()

    cols0 = (rad - width) * (1 - h)
    cross = band_t[pl.ds(pl.multiple_of(srows - halo * h, 16), halo), pl.ds(pl.multiple_of(cols0, 128), width)]

    def cross_plane(k, c):
        xk = x_ref[k, pl.ds(pl.multiple_of(cols0, 128), width), :]
        xsend[k] = nn_dot(cross, xk).astype(BF16)
        return c

    lax.fori_loop(0, planes, cross_plane, 0)

    pl.semaphore_wait(barrier, len(peers))

    def remote(src, dst, send, recv, where):
        return pltpu.make_async_remote_copy(
            src_ref=src, dst_ref=dst, send_sem=send, recv_sem=recv, device_id=where, device_id_type=MESH
        )

    xcopy = remote(xsend, xrecv, s_xs, s_xr, {"span": other})
    xcopy.start()

    def pass_on(k):
        for where in (ahead, behind):
            pl.semaphore_signal(token.at[k], inc=1, device_id={"pitch": where}, device_id_type=MESH)

    pass_on(0)

    ana = ana_ref[...]

    def own_plane(k, c):
        own = band_t[pl.ds(pl.multiple_of(h * srows, 16), srows), :]
        mk = nn_dot(own, x_ref[k]).astype(BF16)
        part[pl.ds(pl.multiple_of(k * srows, 16), srows), :] = nt_dot(mk, ana)
        return c

    lax.fori_loop(0, planes, own_plane, 0)
    tail = part.shape[0] - planes * srows
    if tail:
        part[planes * srows :, :] = jnp.zeros((tail, part.shape[1]), F32)
    pl.semaphore_wait(token.at[0], 2)
    pass_on(1)
    xcopy.wait_recv()
    b0 = (srows - halo) * (1 - h)

    def add_plane(k, c):
        rows = pl.ds(pl.multiple_of(k * srows + b0, 16), halo)
        part[rows, :] = part[rows, :] + nt_dot(xrecv[k], ana)
        return c

    lax.fori_loop(0, planes, add_plane, 0)

    pl.semaphore_wait(token.at[1], 2)

    def rows_of(c, j):
        return pl.ds(pl.multiple_of(c * chunk + j * sub, 16), sub)

    def send_r(s, k, j):
        return remote(
            sb_r.at[s, k, j], rb_r.at[s, k, j], s_sr.at[s, k, j], s_rr.at[s, k, j], {"pitch": right})

    def send_l(s, k, j):
        return remote(
            sb_l.at[s, k, j], rb_l.at[s, k, j], s_sl.at[s, k, j], s_rl.at[s, k, j], {"pitch": left})

    def first_r(k):
        return 1 if k == 1 else 0

    for s in range(reach):
        for k, off in enumerate(offsets):
            for j in range(subs):
                if s >= first_r(k):
                    value = part[rows_of(at(reach - s - off), j), :]
                    if s > first_r(k):
                        send_r(s - 1, k, j).wait_recv()
                        value = value + rb_r[s - 1, k, j].astype(F32)
                    sb_r[s, k, j] = value.astype(BF16)
                    send_r(s, k, j).start()
                value = part[rows_of(at(s - reach - off), j), :]
                if s > 0:
                    send_l(s - 1, k, j).wait_recv()
                    value = value + rb_l[s - 1, k, j].astype(F32)
                sb_l[s, k, j] = value.astype(BF16)
                send_l(s, k, j).start()

    def to_owner(k, j):
        where = {"row": partner, "pitch": at(-offsets[k])}
        return remote(sums.at[k, j], from_roots.at[k, j], e_s.at[k, j], e_r.at[k, j], where)

    for k, off in enumerate(offsets):
        for j in range(subs):
            value = part[rows_of(at(-off), j), :]
            send_l(reach - 1, k, j).wait_recv()
            value = value + rb_l[reach - 1, k, j].astype(F32)
            if reach - 1 >= first_r(k):
                send_r(reach - 1, k, j).wait_recv()
                value = value + rb_r[reach - 1, k, j].astype(F32)
            sums[k, j] = value.astype(BF16)
            to_owner(k, j).start()

    def to_root(k, j, incoming=False):
        c = gath.at[at(-offsets[k]), j] if incoming else gath.at[z, j]
        return remote(c, c, g_s.at[k, j], g_r.at[k, j], {"pitch": at(offsets[k])})

    def fwd_r(s, k, j, incoming=False):
        c = gath.at[at(-s - (1 if incoming else 0) - offsets[k]), j]
        return remote(c, c, a_sr.at[s, k, j], a_rr.at[s, k, j], {"pitch": right})

    def fwd_l(s, k, j, incoming=False):
        c = gath.at[at(s + (1 if incoming else 0) - offsets[k]), j]
        return remote(c, c, a_sl.at[s, k, j], a_rl.at[s, k, j], {"pitch": left})

    def last_l(k):
        return reach - 2 if k == 1 else reach - 1

    for j in range(subs):
        for k in (2, 0, 1):
            to_owner(k, j).wait_recv()
        total = from_roots[2, j].astype(F32) + from_roots[0, j].astype(F32) + from_roots[1, j].astype(F32)
        place = z * chunk + j * sub + lax.broadcasted_iota(jnp.int32, total.shape, 0)
        first = place < half * srows
        cosine = jnp.where(first, rot_ref[0, 0:1, :], rot_ref[0, 1:2, :])
        sine = jnp.where(first, rot_ref[1, 0:1, :], rot_ref[1, 1:2, :])
        swapped = pltpu.roll(total, total.shape[1] // 2, 1)
        gath[z, j] = (total * cosine + swapped * sine).astype(BF16)
        to_root(0, j).start()
        to_root(1, j).start()
        fwd_r(0, 2, j).start()
        fwd_l(0, 2, j).start()

    syn = syn_ref[...]

    def written(c):
        rows = pl.ds(pl.multiple_of(c * chunk, 16), chunk)
        return pltpu.make_async_copy(out_ref.at[rows], out_hbm.at[rows], s_out.at[c])

    def emit(c):
        for j in range(subs):
            out_ref[rows_of(c, j), :] = nn_dot(gath[c, j], syn).astype(BF16)
        written(c).start()

    emit(z)

    def take(k, s):
        ready = []
        if s == 0:
            for j in range(subs):
                to_root(k, j, True).wait_recv()
                fwd_r(0, k, j).start()
                if last_l(k) >= 0:
                    fwd_l(0, k, j).start()
            ready.append(at(-offsets[k]))
        else:
            for j in range(subs):
                fwd_r(s - 1, k, j, True).wait_recv()
                if s < reach:
                    fwd_r(s, k, j).start()
                if s - 1 <= last_l(k):
                    fwd_l(s - 1, k, j, True).wait_recv()
                    if s <= last_l(k):
                        fwd_l(s, k, j).start()
            ready.append(at(-s - offsets[k]))
            if s - 1 <= last_l(k):
                ready.append(at(s - offsets[k]))
        return ready

    lag = min(LAG, reach)
    for t in range(1, reach + lag + 1):
        ready = []
        if t <= reach:
            ready += take(2, t)
        if t >= lag:
            ready += take(0, t - lag)
            ready += take(1, t - lag)
        for c in ready:
            emit(c)

    xcopy.wait_send()
    for k in range(3):
        for j in range(subs):
            to_owner(k, j).wait_send()
            if k < 2:
                to_root(k, j).wait_send()
            for s in range(reach):
                if s >= first_r(k):
                    send_r(s, k, j).wait_send()
                send_l(s, k, j).wait_send()
                fwd_r(s, k, j).wait_send()
                if s <= last_l(k):
                    fwd_l(s, k, j).wait_send()

    def finish(c, carry):
        written(c).wait()
        return carry

    lax.fori_loop(0, n, finish, 0)


def body(outlet, remap_weight, band_start, blade_counts, mode_orders):
    row_count = lax.axis_size("row")
    n = lax.axis_size("pitch")
    planes = outlet[0]
    inst, fields, rad, pitch = planes.shape
    harm = mode_orders.shape[0]
    cols = 2 * harm
    stator = remap_weight.shape[1]
    srows = stator // 2
    nplanes = inst * fields
    halo = 112
    nrows = nplanes * srows
    chunk = -(-nrows // (n * 16)) * 16
    subs = SUBS if chunk % (16 * SUBS) == 0 else 1
    sub = chunk // subs
    reach = (n - 2) // 6
    sem = pltpu.SemaphoreType.DMA
    vm = pl.BlockSpec(memory_space=pltpu.VMEM)
    out = pl.pallas_call(
        functools.partial(kernel, n, row_count, chunk, subs, halo, fields, srows),
        out_shape=jax.ShapeDtypeStruct((n * chunk, pitch), BF16),
        in_specs=[pl.BlockSpec(memory_space=pltpu.HBM)] * 5,
        out_specs=pl.BlockSpec(memory_space=pltpu.HBM),
        scratch_shapes=[
            pltpu.VMEM((nplanes, rad, pitch), BF16),
            pltpu.VMEM((rad, stator), BF16),
            pltpu.VMEM((stator,), jnp.int32),
            pltpu.SMEM((2,), jnp.int32),
            pltpu.VMEM((2, harm), jnp.int32),
            pltpu.VMEM((n * chunk, pitch), BF16),
            pltpu.VMEM((stator, rad), BF16),
            pltpu.VMEM((cols, pitch), BF16),
            pltpu.VMEM((cols, pitch), BF16),
            pltpu.VMEM((2, 128, cols), F32),
            pltpu.VMEM((n * chunk, cols), F32),
            pltpu.VMEM((nplanes, halo, pitch), BF16),
            pltpu.VMEM((nplanes, halo, pitch), BF16),
            pltpu.VMEM((reach, 3, subs, sub, cols), BF16),
            pltpu.VMEM((reach, 3, subs, sub, cols), BF16),
            pltpu.VMEM((reach, 3, subs, sub, cols), BF16),
            pltpu.VMEM((reach, 3, subs, sub, cols), BF16),
            pltpu.VMEM((3, subs, sub, cols), BF16),
            pltpu.VMEM((3, subs, sub, cols), BF16),
            pltpu.VMEM((n, subs, sub, cols), BF16),
            sem((reach, 3, subs)),
            sem((reach, 3, subs)),
            sem((reach, 3, subs)),
            sem((reach, 3, subs)),
            sem,
            sem,
            sem((3, subs)),
            sem((3, subs)),
            sem((2, subs)),
            sem((2, subs)),
            sem((reach, 3, subs)),
            sem((reach, 3, subs)),
            sem((reach, 3, subs)),
            sem((reach, 3, subs)),
            sem((5,)),
            sem((n,)),
            pltpu.SemaphoreType.REGULAR((2,)),
        ],
        compiler_params=pltpu.CompilerParams(
            collective_id=0, has_side_effects=True, vmem_limit_bytes=63 * 1024 * 1024
        ),
    )(
        planes.reshape(nplanes, rad, pitch),
        remap_weight,
        band_start,
        blade_counts,
        mode_orders.T,
    )
    return out[:nrows].reshape(1, inst, fields, srows, pitch)


def solution(mesh):
    placed = (P("row", None, None, "span", "pitch"), P("span", None), P(), P(), P())
    return jax.shard_map(
        body, mesh=mesh, in_specs=placed,
        out_specs=P("row", None, None, "span", "pitch"), check_vma=False)
```

time: 112 us -> 100 us (0.89)
  the two profiles are of different devices: /device:TPU:8 before, /device:TPU:16 now
where the time goes in v3:
time: 100 us
  Pallas kernels  97.9 us (98%)
  local copies, waits for them, and re-layouts  2.34 us (2%)
    pallas_call x1, Pallas kernels, body(): pl.pallas_call(functools.partial(kernel, n, row_count, chunk, subs, halo,...  97.9 us
    slice x1, local copies, waits for them, and re-layouts, body(): return out[:nrows].reshape(1, inst, fields, srows, pitch)  2.34 us

profile of v3, /device:TPU:16, one launch (start us, length us, event | category | flops | bytes accessed | tf_op | source)
XLA Modules:
  0.0 100.2 jit_solution(15365024490992221348)
XLA Ops:
  0.0 97.9 %shard_map.55 = bf16[4608,128]{1,0:T(8,128)(2,1)} custom-call(bf16[10,512,128]{2,1,0:T(8,128)(2,1)} %bitcast.3, bf16[512,896]{1,0:T(8,128)(2,1)} %w_hbm.1, s32[896]{0:T(1024)} %start_hbm.1, s32[2]{0:T(128)} %blade_hbm.1, s32[2,64]{1,0:T(2,128)} %bitcast.4), custom_call_target="tpu_custom_call" | custom-call | tf_op jit(solution)/shard_map/pallas_call | solution.py:332
  97.9 2.3 %slice.3 = bf16[4480,128]{1,0:T(8,128)(2,1)} slice(bf16[4608,128]{1,0:T(8,128)(2,1)} %shard_map.55), slice={[0:4480], [0:128]} | slice | bytes 2293760 | tf_op jit(solution)/shard_map/slice | solution.py:386
